TPU v7x, 128 devices: a whole 4x4x4 slice. The times are simulated.
128 devices in a mesh: rows: 4 (over x), cols: 32 (over y, z, core).
Axes of the slice: x: 4, y: 4, z: 4, core: 2. Of those that a mesh axis runs over, the one named last changes fastest.
Arguments:
- weight: bfloat16 [8192, 16384], P('rows', 'cols'), may hold values from -0.046875 to 0.046875
- hess_inv: float32 [16384, 16384], P('rows', 'cols'), as said below
- selected: int32 [3, 64], replicated, may hold values from 0 to 16383, as said below
- block_mask: int32 [8192, 128], P('rows'), may hold values 0 or 1
- row_limits: int32 [8192], P('rows'), may hold values from 16 to 128
- calibration: bfloat16 [1024, 16384], P(None, 'cols'), may hold values from -6 to 6
Outputs:
- pruned: bfloat16 [8192, 16384], P('rows', 'cols')
- layer_error: float32 [8192, 1024], P('rows', 'cols')
Inputs may be any that keep to these rules, and one draw needn't show every extreme that they name: `selected`: all 192 entries differ; 0 and 16383 are among them. `hess_inv`: symmetric positive definite.
All inputs are finite; a program needn't handle non-finite values. No bound on the sum of `block_mask` on one device may be relied on, other than what follows from the above.
Results may differ from a plain program's by a relative error of at most 0.005.
Values may be sent and summed in bfloat16 or wider, within the bound.
A program may use at most 128 MiB of HBM per device.

v0:
```python
import jax
import jax.numpy as jnp
from jax import lax
from jax.sharding import PartitionSpec as P

STEPS = 3
BLK = 128


def local(weight, hess_inv, selected, block_mask, row_limits, calibration):
    rows_local, cols_local = hess_inv.shape
    out_local = weight.shape[0]
    row_offset = lax.axis_index("rows") * rows_local
    col_offset = lax.axis_index("cols") * cols_local
    refit = weight.astype(jnp.float32)
    inverse = hess_inv
    for iteration in range(STEPS):
        chosen = selected[iteration]
        row_place = chosen - row_offset
        row_inside = (row_place >= 0) & (row_place < rows_local)
        row_pick = jnp.where(
            row_inside[:, None],
            jnp.take(inverse, jnp.clip(row_place, 0, rows_local - 1), axis=0),
            0.0,
        )
        panel = lax.psum(row_pick, "rows")
        col_place = chosen - col_offset
        col_inside = (col_place >= 0) & (col_place < cols_local)
        col_index = jnp.clip(col_place, 0, cols_local - 1)
        inverse_pick = jnp.where(col_inside[None, :], jnp.take(inverse, col_index, axis=1), 0.0)
        refit_pick = jnp.where(col_inside[None, :], jnp.take(refit, col_index, axis=1), 0.0)
        square_pick = jnp.where(col_inside[None, :], jnp.take(panel, col_index, axis=1), 0.0)
        inverse_cols, refit_cols, square = lax.psum((inverse_pick, refit_pick, square_pick), "cols")
        factor = jnp.linalg.cholesky(square)
        coeffs = jax.scipy.linalg.cho_solve((factor, True), panel)
        refit = refit - jnp.dot(refit_cols, coeffs, precision=lax.Precision.HIGHEST)
        inverse = inverse - jnp.dot(inverse_cols, coeffs, precision=lax.Precision.HIGHEST)
    blocks_local = cols_local // BLK
    running_count = jnp.cumsum(block_mask, axis=1)
    retained = block_mask * (running_count <= row_limits[:, None]).astype(jnp.int32)
    own_blocks = lax.dynamic_slice_in_dim(
        retained, lax.axis_index("cols") * blocks_local, blocks_local, 1
    )
    masked = (
        refit.reshape(out_local, blocks_local, BLK) * own_blocks.astype(jnp.float32)[:, :, None]
    ).reshape(out_local, cols_local)
    pruned = masked.astype(jnp.bfloat16)
    difference = (weight.astype(jnp.float32) - masked).astype(jnp.bfloat16)
    widened = lax.all_to_all(difference, "cols", split_axis=0, concat_axis=1, tiled=True)
    row_result = lax.dot_general(
        widened,
        lax.all_gather(calibration, "cols", axis=1, tiled=True),
        (((1,), (1,)), ((), ())),
        preferred_element_type=jnp.float32,
    )
    layer_error = lax.all_to_all(
        row_result.astype(jnp.bfloat16), "cols", split_axis=1, concat_axis=0, tiled=True
    ).astype(row_result.dtype)
    return (pruned, layer_error)


def solution(mesh):
    placed = (
        P("rows", "cols"),
        P("rows", "cols"),
        P(),
        P("rows", None),
        P("rows"),
        P(None, "cols"),
    )
    return jax.shard_map(
        local,
        mesh=mesh,
        in_specs=placed,
        out_specs=(P("rows", "cols"), P("rows", "cols")),
        check_vma=False,
    )
```

profile of v0, /device:TPU:1, one launch (start us, length us, event | category | flops | bytes accessed | tf_op | source)
XLA Modules:
  0.0 925.9 jit_solution(10366670984295173127)
XLA Ops:
  8.9 4.1 gather_fusion.1
  13.8 4.1 copy.56
  22.2 9.0 copy.60
  31.1 4.8 gather_fusion.4
  37.1 19.3 %all-reduce.11.cloned.1.call-done = f32[64,512]{1,0:T(8,128)} async-done(((f32[64,512]{1,0:T(8,128)}), f32[64,512]{1,0:T(8,128)}) %all-reduce.11.cloned.1.call-update) | async-done | bytes 131088 | tf_op jit(solution)/shard_map/psum | solution.py:26
  58.1 123.4 %psum.79 = f32[64,64]{0,1:T(8,128)S(1)} all-reduce(f32[64,64]{0,1:T(8,128)S(1)} %bitcast_select_fusion.7), channel_id=1, replica_groups=mesh['rows'=4,'cols'=32] {'cols'}, use_global_device_ids=true, to_apply=%region_2.6 | all-reduce | flops 4096 | bytes 32768 | tf_op jit(solution)/shard_map/psum | solution.py:33
  181.6 5.8 cholesky.59
  188.7 4.9 custom-call.9
  195.2 6.2 convolution_subtract_fusion.3
  201.4 5.4 copy.59
  211.2 107.3 %all-reduce.19.cloned.1.call-done = (f32[2048,64]{0,1:T(8,128)}, f32[4096,64]{0,1:T(8,128)}) async-done(((f32[2048,64]{0,1:T(8,128)}, f32[4096,64]{0,1:T(8,128)}), (f32[2048,64]{0,1:T(8,128)}, f32[4096,64]{0,1:T(8,128)})) %all-reduce.19.cloned.1.call-update) | async-done | bytes 1572880 | tf_op jit(solution)/shard_map/psum | solution.py:33
  318.4 11.5 %convolution_subtract_fusion.1 = f32[4096,512]{1,0:T(8,128)} fusion(f32[4096,512]{1,0:T(8,128)} %param.18, f32[4096,64]{0,1:T(8,128)} %get-tuple-element.10, f32[64,512]{1,0:T(8,128)S(1)} %fusion.14), kind=kOutput, calls=%fused_computation.12 | convolution fusion | flops 1612709888 | bytes 17956864 | tf_op jit(solution)/shard_map/dot_general | solution.py:37
  330.0 8.9 copy.64
  343.8 4.8 gather_fusion.8
  349.7 33.0 %all-reduce.13.cloned.1.call-done = f32[64,512]{1,0:T(8,128)} async-done(((f32[64,512]{1,0:T(8,128)}), f32[64,512]{1,0:T(8,128)}) %all-reduce.13.cloned.1.call-update) | async-done | bytes 131088 | tf_op jit(solution)/shard_map/psum | solution.py:26
  384.4 123.3 %psum.83 = f32[64,64]{0,1:T(8,128)S(1)} all-reduce(f32[64,64]{0,1:T(8,128)S(1)} %bitcast_select_fusion.6), channel_id=1, replica_groups=mesh['rows'=4,'cols'=32] {'cols'}, use_global_device_ids=true, to_apply=%region_8.15 | all-reduce | flops 4096 | bytes 32768 | tf_op jit(solution)/shard_map/psum | solution.py:33
  507.8 5.8 cholesky.70
  515.0 4.9 custom-call.10
  521.4 6.8 convolution_subtract_fusion.2
  528.2 5.4 copy.63
  538.1 107.3 %all-reduce.17.cloned.1.call-done = (f32[2048,64]{0,1:T(8,128)}, f32[4096,64]{0,1:T(8,128)}) async-done(((f32[2048,64]{0,1:T(8,128)}, f32[4096,64]{0,1:T(8,128)}), (f32[2048,64]{0,1:T(8,128)}, f32[4096,64]{0,1:T(8,128)})) %all-reduce.17.cloned.1.call-update) | async-done | bytes 1572880 | tf_op jit(solution)/shard_map/psum | solution.py:33
  645.4 11.5 %convolution_subtract_fusion = f32[4096,512]{1,0:T(8,128)} fusion(f32[4096,512]{1,0:T(8,128)} %convolution_subtract_fusion.1, f32[4096,64]{0,1:T(8,128)} %get-tuple-element.6, f32[64,512]{1,0:T(8,128)S(1)} %fusion.9), kind=kOutput, calls=%fused_computation.11 | convolution fusion | flops 1612709888 | bytes 17956864 | tf_op jit(solution)/shard_map/dot_general | solution.py:37
  656.9 4.1 gather_fusion.9
  667.2 33.6 %all-reduce.15.cloned.1.call-done = f32[64,512]{1,0:T(8,128)} async-done(((f32[64,512]{1,0:T(8,128)}), f32[64,512]{1,0:T(8,128)}) %all-reduce.15.cloned.1.call-update) | async-done | bytes 131088 | tf_op jit(solution)/shard_map/psum | solution.py:26
  702.5 127.2 %psum.87 = f32[64,64]{0,1:T(8,128)S(1)} all-reduce(f32[64,64]{0,1:T(8,128)S(1)} %bitcast_select_fusion.5), channel_id=1, replica_groups=mesh['rows'=4,'cols'=32] {'cols'}, use_global_device_ids=true, to_apply=%region_12.19 | all-reduce | flops 4096 | bytes 32768 | tf_op jit(solution)/shard_map/psum | solution.py:33
  829.8 5.8 cholesky.81
  837.0 4.9 custom-call.11
  843.5 4.7 mul.27
  848.2 5.5 subtract_convert_fusion
  853.7 36.5 %all_to_all.32 = bf16[32,64,512]{2,1,0:T(8,128)(2,1)S(1)} all-to-all(bf16[32,64,512]{2,1,0:T(8,128)(2,1)S(1)} %bitcast.115), channel_id=1, replica_groups=mesh['rows'=4,'cols'=32] {'cols'}, dimensions={0} | all-to-all | bytes 4194304 | tf_op jit(solution)/shard_map/all_to_all | solution.py:49
  890.5 15.4 %convolution_convert_fusion = bf16[64,1024]{1,0:T(8,128)(2,1)S(1)} fusion(bf16[64,16384]{1,0:T(8,128)(2,1)S(1)} %bitcast.113, bf16[1024,16384]{1,0:T(8,128)(2,1)} %all-gather.2.cloned.1.call-done), kind=kOutput, calls=%fused_computation.17 | convolution fusion | flops 2147549184 | bytes 35782656 | tf_op jit(solution)/shard_map/dot_general | solution.py:50
  906.2 11.4 %all_to_all.33 = bf16[32,2,1024]{2,1,0:T(2,128)(2,1)S(1)} all-to-all(bf16[32,2,1024]{2,1,0:T(2,128)(2,1)S(1)} %reshape.238), channel_id=1, replica_groups=mesh['rows'=4,'cols'=32] {'cols'}, dimensions={0} | all-to-all | bytes 262144 | tf_op jit(solution)/shard_map/all_to_all | solution.py:56
  (85 shorter events, 44.8 us)
Async XLA Ops:
  7.2 49.2 %all-reduce.11.cloned.1.call-start = ((), (), s32[]{:S(2)}) async-start(), calls=%async_computation.3 | async-start | bytes 262144 | tf_op jit(solution)/shard_map/psum | solution.py:26
  13.7 181.4 %all-reduce.9.cloned.1.call-start = ((), (), s32[]{:S(2)}) async-start(), calls=%async_computation.2 | async-start | bytes 1048576 | tf_op jit(solution)/shard_map/psum | solution.py:33
  22.1 296.3 %all-reduce.19.cloned.1.call-start = ((), (), s32[]{:S(2)}) async-start(), calls=%async_computation.8 | async-start | bytes 3145728 | tf_op jit(solution)/shard_map/psum | solution.py:33
  35.9 159.3 %copy-start.1 = (bf16[2048,512]{1,0:T(8,128)(2,1)S(1)}, bf16[2048,512]{1,0:T(8,128)(2,1)}, u32[]{:S(2)}) copy-start(bf16[2048,512]{1,0:T(8,128)(2,1)} %param.17) | copy-start | bytes 6291460
  210.9 171.8 %all-reduce.13.cloned.1.call-start = ((), (), s32[]{:S(2)}) async-start(), calls=%async_computation.4 | async-start | bytes 262144 | tf_op jit(solution)/shard_map/psum | solution.py:26
  343.8 301.6 %all-reduce.17.cloned.1.call-start = ((), (), s32[]{:S(2)}) async-start(), calls=%async_computation.7 | async-start | bytes 3145728 | tf_op jit(solution)/shard_map/psum | solution.py:33
  537.8 163.0 %all-reduce.15.cloned.1.call-start = ((), (), s32[]{:S(2)}) async-start(), calls=%async_computation.5 | async-start | bytes 262144 | tf_op jit(solution)/shard_map/psum | solution.py:26
  656.9 9.0 copy-start.3
  661.8 228.7 %all-gather.2.cloned.1.call-start = ((), (), s32[]{:S(2)}) async-start(), calls=%async_computation.6 | async-start | bytes 34603008 | tf_op jit(solution)/shard_map/all_gather | solution.py:52
  841.9 6.4 copy-start
  841.9 6.4 copy-start.2
Sparse Core Ops, SparseCore 0:
  13.8 42.4 all-reduce.10
  59.6 107.1 all-reduce.8
  211.0 107.3 all-reduce.18
  343.9 38.7 all-reduce.12
  537.9 107.4 all-reduce.16
  661.9 38.8 all-reduce.14
  703.0 128.8 all-gather.1
where the time goes:
time: 927 us; the launch traced here: 926 us
  blocking collectives  422 us (46%)
  waiting for transfers between devices  301 us (32%)
  local copies, waits for them, and re-layouts  77.9 us (8%)
  matrix products  61.5 us (7%)
  other arithmetic  48.2 us (5%)
  between operations  14.5 us (2%)
    psum x3, blocking collectives, local(): lax.psum((inverse_pick, refit_pick, square_pick), 'cols')  374 us
    psum x3, waiting for transfers between devices, local(): lax.psum((inverse_pick, refit_pick, square_pick), 'cols')  215 us
    psum x3, waiting for transfers between devices, local(): panel = lax.psum(row_pick, 'rows')  85.9 us
    all_to_all x1, blocking collectives, local(): lax.all_to_all(difference, 'cols', split_axis=0, concat_axis=1, tiled=True)  36.5 us
    dot_general x2, matrix products, local(): jnp.dot(inverse_cols, coeffs, precision=lax.Precision.HIGHEST)  23.1 us
    another operation x9, other arithmetic, local(): factor = jnp.linalg.cholesky(square)  19.6 us
  transfers between devices with their start and end apart: 7, of which 5 were waited for; matrix products, arithmetic and copies ran while one was open for 8% of the time, Pallas kernels for 0%

commit v1 on v0

--- a/solution.py
+++ b/solution.py
@@ -23,7 +23,7 @@
             jnp.take(inverse, jnp.clip(row_place, 0, rows_local - 1), axis=0),
             0.0,
         )
-        panel = lax.psum(row_pick, "rows")
+        panel = jnp.sum(lax.all_gather(row_pick, "rows"), axis=0)
         col_place = chosen - col_offset
         col_inside = (col_place >= 0) & (col_place < cols_local)
         col_index = jnp.clip(col_place, 0, cols_local - 1)

time: 927 us -> 866 us (0.934)
  waiting for transfers between devices: 301 us -> 209 us
  blocking collectives: 422 us -> 457 us
    psum x3 -> x0, waiting for transfers between devices: 85.9 us -> none  [local(): panel = lax.psum(row_pick, 'rows')]
    all_gather x0 -> x3, blocking collectives: none -> 35.6 us  [local(): panel = jnp.sum(lax.all_gather(row_pick, 'rows'), axis=0)]
  transfers between devices with their start and end apart: 7 -> 4, of which waited for: 5 -> 2; matrix products, arithmetic and copies ran while one was open for 8% -> 9% of each run, Pallas kernels for 0% -> 0%
where the time goes in v1:
time: 866 us; the launch traced here: 864 us
  blocking collectives  457 us (53%)
  waiting for transfers between devices  209 us (24%)
  local copies, waits for them, and re-layouts  76.4 us (9%)
  matrix products  58.6 us (7%)
  other arithmetic  48.3 us (6%)
  between operations  14.2 us (2%)
    psum x3, blocking collectives, local(): lax.psum((inverse_pick, refit_pick, square_pick), 'cols')  373 us
    psum x3, waiting for transfers between devices, local(): lax.psum((inverse_pick, refit_pick, square_pick), 'cols')  209 us
    all_to_all x1, blocking collectives, local(): lax.all_to_all(difference, 'cols', split_axis=0, concat_axis=1, tiled=True)  36.6 us
    all_gather x3, blocking collectives, local(): panel = jnp.sum(lax.all_gather(row_pick, 'rows'), axis=0)  35.6 us
    dot_general x2, matrix products, local(): jnp.dot(inverse_cols, coeffs, precision=lax.Precision.HIGHEST)  23 us
    another operation x9, other arithmetic, local(): factor = jnp.linalg.cholesky(square)  19.6 us
    dot_general x3, matrix products, local(): refit = refit - jnp.dot(refit_cols, coeffs, precision=lax.Precision.HIGHEST)  18.5 us
  transfers between devices with their start and end apart: 4, of which 2 were waited for; matrix products, arithmetic and copies ran while one was open for 9% of the time, Pallas kernels for 0%

profile of v1, /device:TPU:1, one launch (start us, length us, event | category | flops | bytes accessed | tf_op | source)
XLA Modules:
  0.0 864.2 jit_solution(348549514732969949)
XLA Ops:
  8.8 4.1 copy.47
  17.2 8.9 %copy.51 = f32[4096,512]{0,1:T(8,128)} copy(f32[4096,512]{1,0:T(8,128)} %param.18) | data formatting | bytes 16777216 | tf_op args[1]
  26.2 4.1 gather_fusion.1
  30.4 12.4 %all-gather = f32[256,512]{1,0:T(8,128)S(1)} all-gather(f32[64,512]{1,0:T(8,128)S(1)} %select_select_fusion.2), channel_id=2, replica_groups=mesh['rows'=4,'cols'=32] {'rows'}, dimensions={0}, use_global_device_ids=true | all-gather | bytes 655360 | tf_op jit(solution)/shard_map/all_gather | solution.py:26
  43.7 124.6 %psum.57 = f32[64,64]{0,1:T(8,128)S(1)} all-reduce(f32[64,64]{0,1:T(8,128)S(1)} %bitcast_select_fusion.7), channel_id=1, replica_groups=mesh['rows'=4,'cols'=32] {'cols'}, use_global_device_ids=true, to_apply=%region_2.6 | all-reduce | flops 4096 | bytes 32768 | tf_op jit(solution)/shard_map/psum | solution.py:33
  168.4 5.8 cholesky.59
  175.5 4.9 custom-call.9
  180.8 4.9 gather_fusion.4
  187.2 6.2 convolution_subtract_fusion.3
  193.4 5.4 copy.50
  203.1 106.4 %all-reduce.10.cloned.1.call-done = (f32[2048,64]{0,1:T(8,128)}, f32[4096,64]{0,1:T(8,128)}) async-done(((f32[2048,64]{0,1:T(8,128)}, f32[4096,64]{0,1:T(8,128)}), (f32[2048,64]{0,1:T(8,128)}, f32[4096,64]{0,1:T(8,128)})) %all-reduce.10.cloned.1.call-update) | async-done | bytes 1572880 | tf_op jit(solution)/shard_map/psum | solution.py:33
  309.6 11.5 %convolution_subtract_fusion.1 = f32[4096,512]{1,0:T(8,128)} fusion(f32[4096,512]{1,0:T(8,128)} %param.18, f32[4096,64]{0,1:T(8,128)} %get-tuple-element.10, f32[64,512]{1,0:T(8,128)S(1)} %fusion.14), kind=kOutput, calls=%fused_computation.12 | convolution fusion | flops 1612709888 | bytes 17956864 | tf_op jit(solution)/shard_map/dot_general | solution.py:37
  321.1 8.9 %copy.55 = f32[4096,512]{0,1:T(8,128)} copy(f32[4096,512]{1,0:T(8,128)} %convolution_subtract_fusion.1) | data formatting | bytes 16777216 | tf_op jit(solution)/shard_map/sub | solution.py:37
  334.2 11.4 %all-gather.1 = f32[256,512]{1,0:T(8,128)S(1)} all-gather(f32[64,512]{1,0:T(8,128)S(1)} %select_select_fusion.1), channel_id=3, replica_groups=mesh['rows'=4,'cols'=32] {'rows'}, dimensions={0}, use_global_device_ids=true | all-gather | bytes 655360 | tf_op jit(solution)/shard_map/all_gather | solution.py:26
  346.5 122.2 %psum.60 = f32[64,64]{0,1:T(8,128)S(1)} all-reduce(f32[64,64]{0,1:T(8,128)S(1)} %bitcast_select_fusion.6), channel_id=1, replica_groups=mesh['rows'=4,'cols'=32] {'cols'}, use_global_device_ids=true, to_apply=%region_8.15 | all-reduce | flops 4096 | bytes 32768 | tf_op jit(solution)/shard_map/psum | solution.py:33
  468.8 5.8 cholesky.70
  476.0 4.9 custom-call.10
  481.5 6.8 convolution_subtract_fusion.2
  488.3 5.4 copy.54
  493.7 4.8 gather_fusion.8
  509.0 102.4 %all-reduce.8.cloned.1.call-done = (f32[2048,64]{0,1:T(8,128)}, f32[4096,64]{0,1:T(8,128)}) async-done(((f32[2048,64]{0,1:T(8,128)}, f32[4096,64]{0,1:T(8,128)}), (f32[2048,64]{0,1:T(8,128)}, f32[4096,64]{0,1:T(8,128)})) %all-reduce.8.cloned.1.call-update) | async-done | bytes 1572880 | tf_op jit(solution)/shard_map/psum | solution.py:33
  611.4 11.5 %convolution_subtract_fusion = f32[4096,512]{1,0:T(8,128)} fusion(f32[4096,512]{1,0:T(8,128)} %convolution_subtract_fusion.1, f32[4096,64]{0,1:T(8,128)} %get-tuple-element.6, f32[64,512]{1,0:T(8,128)S(1)} %fusion.9), kind=kOutput, calls=%fused_computation.11 | convolution fusion | flops 1612709888 | bytes 17956864 | tf_op jit(solution)/shard_map/dot_general | solution.py:37
  622.9 4.6 gather_fusion.9
  627.6 11.8 %all-gather.2 = f32[256,512]{1,0:T(8,128)} all-gather(f32[64,512]{1,0:T(8,128)S(1)} %select_select_fusion), channel_id=4, replica_groups=mesh['rows'=4,'cols'=32] {'rows'}, dimensions={0}, use_global_device_ids=true | all-gather | bytes 655360 | tf_op jit(solution)/shard_map/all_gather | solution.py:26
  642.7 126.5 %psum.63 = f32[64,64]{0,1:T(8,128)S(1)} all-reduce(f32[64,64]{0,1:T(8,128)S(1)} %bitcast_select_fusion.5), channel_id=1, replica_groups=mesh['rows'=4,'cols'=32] {'cols'}, use_global_device_ids=true, to_apply=%region_12.19 | all-reduce | flops 4096 | bytes 32768 | tf_op jit(solution)/shard_map/psum | solution.py:33
  769.4 5.8 cholesky.81
  776.5 4.9 custom-call.11
  782.1 4.7 mul.27
  786.8 5.5 subtract_convert_fusion
  792.2 36.6 %all_to_all.32 = bf16[32,64,512]{2,1,0:T(8,128)(2,1)S(1)} all-to-all(bf16[32,64,512]{2,1,0:T(8,128)(2,1)S(1)} %bitcast.118), channel_id=1, replica_groups=mesh['rows'=4,'cols'=32] {'cols'}, dimensions={0} | all-to-all | bytes 4194304 | tf_op jit(solution)/shard_map/all_to_all | solution.py:49
  829.0 15.4 %convolution_convert_fusion = bf16[64,1024]{1,0:T(8,128)(2,1)S(1)} fusion(bf16[64,16384]{1,0:T(8,128)(2,1)S(1)} %bitcast.116, bf16[1024,16384]{1,0:T(8,128)(2,1)} %all-gather.5.cloned.1.call-done), kind=kOutput, calls=%fused_computation.17 | convolution fusion | flops 2147549184 | bytes 35782656 | tf_op jit(solution)/shard_map/dot_general | solution.py:50
  844.8 11.4 %all_to_all.33 = bf16[32,2,1024]{2,1,0:T(2,128)(2,1)S(1)} all-to-all(bf16[32,2,1024]{2,1,0:T(2,128)(2,1)S(1)} %reshape.241), channel_id=1, replica_groups=mesh['rows'=4,'cols'=32] {'cols'}, dimensions={0} | all-to-all | bytes 262144 | tf_op jit(solution)/shard_map/all_to_all | solution.py:56
  (82 shorter events, 39.3 us)
Async XLA Ops:
  7.2 180.0 %all-reduce.6.cloned.1.call-start = ((), (), s32[]{:S(2)}) async-start(), calls=%async_computation.2 | async-start | bytes 1048576 | tf_op jit(solution)/shard_map/psum | solution.py:33
  17.2 292.4 %all-reduce.10.cloned.1.call-start = ((), (), s32[]{:S(2)}) async-start(), calls=%async_computation.5 | async-start | bytes 3145728 | tf_op jit(solution)/shard_map/psum | solution.py:33
  180.8 6.4 copy-start.1
  202.9 408.5 %all-reduce.8.cloned.1.call-start = ((), (), s32[]{:S(2)}) async-start(), calls=%async_computation.4 | async-start | bytes 3145728 | tf_op jit(solution)/shard_map/psum | solution.py:33
  502.8 5.0 copy-start.3
  503.8 325.2 %all-gather.5.cloned.1.call-start = ((), (), s32[]{:S(2)}) async-start(), calls=%async_computation.3 | async-start | bytes 34603008 | tf_op jit(solution)/shard_map/all_gather | solution.py:52
  781.4 5.3 copy-start
  781.5 5.3 copy-start.2
Sparse Core Ops, SparseCore 0:
  17.3 107.8 all-reduce.5
  203.0 106.5 all-reduce.9
  503.9 107.4 all-reduce.7
  613.4 125.5 all-gather.4
